TPU v7x, 32 devices: a whole 2x2x4 slice. The times are simulated.
32 devices in a mesh: hi: 4 (over x, core), lo: 8 (over z, y).
Axes of the slice: x: 2, y: 2, z: 4, core: 2. Of those that a mesh axis runs over, the one named last changes fastest.
Arguments:
- queries: bfloat16 [4096, 512], P(('hi', 'lo')), may hold values from -50 to 50
- key_rows: bfloat16 [4096, 128], P(('hi', 'lo')), may hold values from -6 to 6
- value_rows: bfloat16 [4096, 128], P(('hi', 'lo')), may hold values from -6 to 6
- global_positions: int32 [32, 8], P(('hi', 'lo')), may hold values from 0 to 127, as said below
Outputs:
- attended: bfloat16 [4096, 512], P(('hi', 'lo'))
Inputs may be any that keep to these rules, and one draw needn't show every extreme that they name: `global_positions`: each row holds 8 distinct positions within a block.
All inputs are finite; a program needn't handle non-finite values.
Results may differ from a plain program's by a relative error of at most 0.0045.
Values may be sent and summed in bfloat16 or wider, within the bound.
A program may use at most 64 MiB of HBM per device.

v0:
```python
import jax
import jax.numpy as jnp
from jax import lax
from jax.sharding import PartitionSpec as P


def from_partner(value, axis, distance):
    mask = 2**distance
    pairs = [(source, source ^ mask) for source in range(lax.axis_size(axis))]
    return lax.ppermute(value, axis, pairs)


def attend(state_now, grouped, key_part, value_part):
    running, denominator, numerator = state_now
    score_scale = key_part.shape[1] ** (-0.5)
    row_total = key_part.shape[0]
    for begin in range(0, row_total, 1024):
        finish = min(begin + 1024, row_total)
        key_slice = key_part[begin:finish]
        value_slice = value_part[begin:finish]
        scores = (
            jnp.einsum("qhd,kd->hqk", grouped, key_slice, preferred_element_type=jnp.float32)
            * score_scale
        )
        fresh = jnp.maximum(running, jnp.max(scores, axis=2))
        weights = jnp.exp(scores - fresh[:, :, None])
        factor = jnp.exp(running - fresh)
        denominator = denominator * factor + jnp.sum(weights, axis=2)
        update = jnp.einsum(
            "hqk,kd->qhd",
            weights.astype(jnp.bfloat16),
            value_slice,
            preferred_element_type=jnp.float32,
        )
        numerator = numerator * jnp.transpose(factor)[:, :, None] + update
        running = fresh
    return (running, denominator, numerator)


def lo_pair_rows(payload, bit_index):
    return from_partner((payload[0], payload[1], payload[2], payload[3]), "lo", bit_index)


def hi_pair_rows(payload, bit_index):
    return from_partner((payload[0], payload[1], payload[2], payload[3]), "hi", bit_index)


def local(queries, key_rows, value_rows, global_positions):
    block_rows, head_width = key_rows.shape
    head_count = queries.shape[1] // head_width
    grouped = queries.reshape(block_rows, head_count, head_width)
    state_now = (
        jnp.full((head_count, block_rows), -jnp.inf, jnp.float32),
        jnp.zeros((head_count, block_rows), jnp.float32),
        jnp.zeros((block_rows, head_count, head_width), jnp.float32),
    )
    state_now = attend(state_now, grouped, key_rows, value_rows)
    picked_keys = jnp.take(key_rows, global_positions[0], axis=0)
    picked_values = jnp.take(value_rows, global_positions[0], axis=0)
    lo_bits = lax.axis_size("lo").bit_length() - 1
    hi_bits = lax.axis_size("hi").bit_length() - 1
    lo_sections = [(0, bit_index) for bit_index in range(lo_bits)]
    hi_sections = [(1, bit_index) for bit_index in range(hi_bits)]
    sections = lo_sections + hi_sections
    held_keys, held_values = (picked_keys, picked_values)
    state_now = attend(state_now, grouped, held_keys, held_values)
    for axis_pick, bit_index in sections:
        payload = (key_rows, value_rows, held_keys, held_values)
        if axis_pick == 0:
            arrived = lo_pair_rows(payload, bit_index)
        else:
            arrived = hi_pair_rows(payload, bit_index)
        state_now = attend(state_now, grouped, arrived[0], arrived[1])
        state_now = attend(state_now, grouped, arrived[2], arrived[3])
        held_keys = jnp.concatenate([held_keys, arrived[2]], axis=0)
        held_values = jnp.concatenate([held_values, arrived[3]], axis=0)
    running, denominator, numerator = state_now
    result = numerator / jnp.transpose(denominator)[:, :, None]
    return result.reshape(block_rows, head_count * head_width).astype(jnp.bfloat16)


def solution(mesh):
    return jax.shard_map(
        local,
        mesh=mesh,
        in_specs=(
            P(("hi", "lo"), None),
            P(("hi", "lo"), None),
            P(("hi", "lo"), None),
            P(("hi", "lo"), None),
        ),
        out_specs=P(("hi", "lo"), None),
        check_vma=False,
    )
```

profile of v0, /device:TPU:0, one launch (start us, length us, event | category | flops | bytes accessed | tf_op | source)
XLA Modules:
  0.0 66.2 jit_solution(8812962944372102103)
XLA Ops:
  0.0 0.9 %copy.9 = bf16[128,128]{0,1:T(8,128)(2,1)S(1)} copy(bf16[128,128]{1,0:T(8,128)(2,1)} %param.8) | data formatting | bytes 65536 | tf_op args[2]
  0.9 3.0 %collective-permute-start.17 = (bf16[128,128]{0,1:T(8,128)(2,1)S(1)}, bf16[128,128]{0,1:T(8,128)(2,1)S(1)}, u32[]{:S(2)}, u32[]{:S(2)}) collective-permute-start(bf16[128,128]{0,1:T(8,128)(2,1)S(1)} %copy.9), channel_id=1, source_target_pairs={{0,16},{8,24},{16,0},{24,8},{1,17},{9,25},{17,1},{25,9},{2,18},{10... | collective-permute-start | bytes 98312 | tf_op jit(solution)/shard_map/ppermute | solution.py:10
  4.0 2.6 %collective-permute-start.9 = (bf16[128,128]{0,1:T(8,128)(2,1)S(1)}, bf16[128,128]{0,1:T(8,128)(2,1)S(1)}, u32[]{:S(2)}, u32[]{:S(2)}) collective-permute-start(bf16[128,128]{0,1:T(8,128)(2,1)S(1)} %copy.9), channel_id=1, source_target_pairs={{0,4},{1,5},{2,6},{3,7},{4,0},{5,1},{6,2},{7,3},{8,12},{9,13},{10,... | collective-permute-start | bytes 98312 | tf_op jit(solution)/shard_map/ppermute | solution.py:10
  6.6 1.6 %collective-permute-start.5 = (bf16[128,128]{0,1:T(8,128)(2,1)S(1)}, bf16[128,128]{0,1:T(8,128)(2,1)S(1)}, u32[]{:S(2)}, u32[]{:S(2)}) collective-permute-start(bf16[128,128]{0,1:T(8,128)(2,1)S(1)} %copy.9), channel_id=1, source_target_pairs={{0,2},{1,3},{2,0},{3,1},{4,6},{5,7},{6,4},{7,5},{8,10},{9,11},{10,... | collective-permute-start | bytes 98312 | tf_op jit(solution)/shard_map/ppermute | solution.py:10
  9.4 1.5 %collective-permute-start.2 = (bf16[8,128]{1,0:T(8,128)(2,1)S(1)}, bf16[8,128]{1,0:T(8,128)(2,1)S(1)}, u32[]{:S(2)}, u32[]{:S(2)}) collective-permute-start(bf16[8,128]{1,0:T(8,128)(2,1)S(1)} %get-tuple-element.39), channel_id=1, source_target_pairs={{0,1},{1,0},{2,3},{3,2},{4,5},{5,4},{6,7},{7,6},{8,9},{9,8},{10,11... | collective-permute-start | bytes 6152 | tf_op jit(solution)/shard_map/ppermute | solution.py:10
  11.4 1.6 %collective-permute-done.2 = bf16[8,128]{1,0:T(8,128)(2,1)S(1)} collective-permute-done((bf16[8,128]{1,0:T(8,128)(2,1)S(1)}, bf16[8,128]{1,0:T(8,128)(2,1)S(1)}, u32[]{:S(2)}, u32[]{:S(2)}) %collective-permute-start.2) | collective-permute-done | bytes 2080 | tf_op jit(solution)/shard_map/ppermute | solution.py:10
  13.0 1.5 %collective-permute-start.3 = (bf16[8,128]{1,0:T(8,128)(2,1)S(1)}, bf16[8,128]{1,0:T(8,128)(2,1)S(1)}, u32[]{:S(2)}, u32[]{:S(2)}) collective-permute-start(bf16[8,128]{1,0:T(8,128)(2,1)S(1)} %get-tuple-element.23), channel_id=1, source_target_pairs={{0,1},{1,0},{2,3},{3,2},{4,5},{5,4},{6,7},{7,6},{8,9},{9,8},{10,11... | collective-permute-start | bytes 6152 | tf_op jit(solution)/shard_map/ppermute | solution.py:10
  14.7 1.9 %collective-permute-done.3 = bf16[8,128]{1,0:T(8,128)(2,1)S(1)} collective-permute-done((bf16[8,128]{1,0:T(8,128)(2,1)S(1)}, bf16[8,128]{1,0:T(8,128)(2,1)S(1)}, u32[]{:S(2)}, u32[]{:S(2)}) %collective-permute-start.3) | collective-permute-done | bytes 2080 | tf_op jit(solution)/shard_map/ppermute | solution.py:10
  17.1 3.1 %collective-permute-done.6 = bf16[16,128]{1,0:T(8,128)(2,1)S(1)} collective-permute-done((bf16[16,128]{1,0:T(8,128)(2,1)S(1)}, bf16[16,128]{1,0:T(8,128)(2,1)S(1)}, u32[]{:S(2)}, u32[]{:S(2)}) %collective-permute-start.6) | collective-permute-done | bytes 4128 | tf_op jit(solution)/shard_map/ppermute | solution.py:10
  20.8 3.0 %collective-permute-done.7 = bf16[16,128]{1,0:T(8,128)(2,1)S(1)} collective-permute-done((bf16[16,128]{1,0:T(8,128)(2,1)S(1)}, bf16[16,128]{1,0:T(8,128)(2,1)S(1)}, u32[]{:S(2)}, u32[]{:S(2)}) %collective-permute-start.7) | collective-permute-done | bytes 4128 | tf_op jit(solution)/shard_map/ppermute | solution.py:10
  24.1 4.2 %collective-permute-done.10 = bf16[32,128]{1,0:T(8,128)(2,1)S(1)} collective-permute-done((bf16[32,128]{1,0:T(8,128)(2,1)S(1)}, bf16[32,128]{1,0:T(8,128)(2,1)S(1)}, u32[]{:S(2)}, u32[]{:S(2)}) %collective-permute-start.10) | collective-permute-done | bytes 8224 | tf_op jit(solution)/shard_map/ppermute | solution.py:10
  28.9 4.0 %collective-permute-done.11 = bf16[32,128]{1,0:T(8,128)(2,1)S(1)} collective-permute-done((bf16[32,128]{1,0:T(8,128)(2,1)S(1)}, bf16[32,128]{1,0:T(8,128)(2,1)S(1)}, u32[]{:S(2)}, u32[]{:S(2)}) %collective-permute-start.11) | collective-permute-done | bytes 8224 | tf_op jit(solution)/shard_map/ppermute | solution.py:10
  32.9 1.2 %collective-permute-done.14 = bf16[64,128]{1,0:T(8,128)(2,1)S(1)} collective-permute-done((bf16[64,128]{1,0:T(8,128)(2,1)S(1)}, bf16[64,128]{1,0:T(8,128)(2,1)S(1)}, u32[]{:S(2)}, u32[]{:S(2)}) %collective-permute-start.14) | collective-permute-done | bytes 16416 | tf_op jit(solution)/shard_map/ppermute | solution.py:10
  34.4 0.8 %collective-permute-done.15 = bf16[64,128]{1,0:T(8,128)(2,1)S(1)} collective-permute-done((bf16[64,128]{1,0:T(8,128)(2,1)S(1)}, bf16[64,128]{1,0:T(8,128)(2,1)S(1)}, u32[]{:S(2)}, u32[]{:S(2)}) %collective-permute-start.15) | collective-permute-done | bytes 16416 | tf_op jit(solution)/shard_map/ppermute | solution.py:10
  35.4 1.0 %collective-permute-done.12 = bf16[128,128]{1,0:T(8,128)(2,1)S(1)} collective-permute-done((bf16[128,128]{1,0:T(8,128)(2,1)S(1)}, bf16[128,128]{1,0:T(8,128)(2,1)S(1)}, u32[]{:S(2)}, u32[]{:S(2)}) %collective-permute-start.12) | collective-permute-done | bytes 32800 | tf_op jit(solution)/shard_map/ppermute | solution.py:10
  37.2 3.2 %collective-permute-done.16 = bf16[128,128]{1,0:T(8,128)(2,1)S(1)} collective-permute-done((bf16[128,128]{1,0:T(8,128)(2,1)S(1)}, bf16[128,128]{1,0:T(8,128)(2,1)S(1)}, u32[]{:S(2)}, u32[]{:S(2)}) %collective-permute-start.16) | collective-permute-done | bytes 32800 | tf_op jit(solution)/shard_map/ppermute | solution.py:10
  40.4 1.5 %collective-permute-start = (bf16[128,128]{1,0:T(8,128)(2,1)S(1)}, bf16[128,128]{1,0:T(8,128)(2,1)S(1)}, u32[]{:S(2)}, u32[]{:S(2)}) collective-permute-start(bf16[128,128]{1,0:T(8,128)(2,1)S(1)} %copy-done.2), channel_id=1, source_target_pairs={{0,1},{1,0},{2,3},{3,2},{4,5},{5,4},{6,7},{7,6},{8,9},{9,8},{10,11... | collective-permute-start | bytes 98312 | tf_op jit(solution)/shard_map/ppermute | solution.py:10
  42.1 2.2 %collective-permute-done = bf16[128,128]{1,0:T(8,128)(2,1)S(1)} collective-permute-done((bf16[128,128]{1,0:T(8,128)(2,1)S(1)}, bf16[128,128]{1,0:T(8,128)(2,1)S(1)}, u32[]{:S(2)}, u32[]{:S(2)}) %collective-permute-start) | collective-permute-done | bytes 32800 | tf_op jit(solution)/shard_map/ppermute | solution.py:10
  45.0 3.3 %collective-permute-done.4 = bf16[128,128]{1,0:T(8,128)(2,1)S(1)} collective-permute-done((bf16[128,128]{1,0:T(8,128)(2,1)S(1)}, bf16[128,128]{1,0:T(8,128)(2,1)S(1)}, u32[]{:S(2)}, u32[]{:S(2)}) %collective-permute-start.4) | collective-permute-done | bytes 32800 | tf_op jit(solution)/shard_map/ppermute | solution.py:10
  48.8 4.5 %collective-permute-done.8 = bf16[128,128]{1,0:T(8,128)(2,1)S(1)} collective-permute-done((bf16[128,128]{1,0:T(8,128)(2,1)S(1)}, bf16[128,128]{1,0:T(8,128)(2,1)S(1)}, u32[]{:S(2)}, u32[]{:S(2)}) %collective-permute-start.8) | collective-permute-done | bytes 32800 | tf_op jit(solution)/shard_map/ppermute | solution.py:10
  54.0 3.2 %collective-permute-done.18 = bf16[128,128]{1,0:T(8,128)(2,1)S(1)} collective-permute-done((bf16[128,128]{1,0:T(8,128)(2,1)S(1)}, bf16[128,128]{1,0:T(8,128)(2,1)S(1)}, u32[]{:S(2)}, u32[]{:S(2)}) %collective-permute-start.18) | collective-permute-done | bytes 32800 | tf_op jit(solution)/shard_map/ppermute | solution.py:10
  58.7 2.4 %collective-permute-done.19 = bf16[128,128]{1,0:T(8,128)(2,1)S(1)} collective-permute-done((bf16[128,128]{1,0:T(8,128)(2,1)S(1)}, bf16[128,128]{1,0:T(8,128)(2,1)S(1)}, u32[]{:S(2)}, u32[]{:S(2)}) %collective-permute-start.19) | collective-permute-done | bytes 32800 | tf_op jit(solution)/shard_map/ppermute | solution.py:10
  61.1 1.5 %collective-permute-start.1 = (bf16[128,128]{0,1:T(8,128)(2,1)S(1)}, bf16[128,128]{0,1:T(8,128)(2,1)S(1)}, u32[]{:S(2)}, u32[]{:S(2)}) collective-permute-start(bf16[128,128]{0,1:T(8,128)(2,1)S(1)} %copy.9), channel_id=1, source_target_pairs={{0,1},{1,0},{2,3},{3,2},{4,5},{5,4},{6,7},{7,6},{8,9},{9,8},{10,11... | collective-permute-start | bytes 98312 | tf_op jit(solution)/shard_map/ppermute | solution.py:10
  65.4 0.8 %copy.30 = bf16[128,512]{1,0:T(8,128)(2,1)} copy(bf16[128,512]{0,1:T(8,128)(2,1)S(1)} %bitcast.450) | data formatting | bytes 262144 | tf_op jit(solution)/shard_map/convert_element_type | solution.py:79
  (81 shorter events, 11.3 us)
Async XLA Ops:
  0.0 10.9 %copy-start = (bf16[128,512]{1,0:T(8,128)(2,1)S(1)}, bf16[128,512]{1,0:T(8,128)(2,1)}, u32[]{:S(2)}) copy-start(bf16[128,512]{1,0:T(8,128)(2,1)} %param.6) | copy-start | bytes 393220
  0.0 8.2 %copy-start.1 = (bf16[128,128]{1,0:T(8,128)(2,1)S(1)}, bf16[128,128]{1,0:T(8,128)(2,1)}, u32[]{:S(2)}) copy-start(bf16[128,128]{1,0:T(8,128)(2,1)} %param.8) | copy-start | bytes 98308
  0.0 8.1 %copy-start.3 = (s32[1,8]{1,0:T(1,128)S(1)}, s32[1,8]{1,0:T(1,128)}, u32[]{:S(2)}) copy-start(s32[1,8]{1,0:T(1,128)} %param.9) | copy-start | bytes 100
  0.0 8.8 %copy-start.2 = (bf16[128,128]{1,0:T(8,128)(2,1)S(1)}, bf16[128,128]{1,0:T(8,128)(2,1)}, u32[]{:S(2)}) copy-start(bf16[128,128]{1,0:T(8,128)(2,1)} %param.7) | copy-start | bytes 98308
  0.9 62.1 %collective-permute-start.17 = (bf16[128,128]{0,1:T(8,128)(2,1)S(1)}, bf16[128,128]{0,1:T(8,128)(2,1)S(1)}, u32[]{:S(2)}, u32[]{:S(2)}) collective-permute-start(bf16[128,128]{0,1:T(8,128)(2,1)S(1)} %copy.9), channel_id=1, source_target_pairs={{0,16},{8,24},{16,0},{24,8},{1,17},{9,25},{17,1},{25,9},{2,18},{10... | collective-permute-start | bytes 98312 | tf_op jit(solution)/shard_map/ppermute | solution.py:10
  4.0 59.5 %collective-permute-start.13 = (bf16[128,128]{0,1:T(8,128)(2,1)S(1)}, bf16[128,128]{0,1:T(8,128)(2,1)S(1)}, u32[]{:S(2)}, u32[]{:S(2)}) collective-permute-start(bf16[128,128]{0,1:T(8,128)(2,1)S(1)} %copy.9), channel_id=1, source_target_pairs={{0,8},{8,0},{16,24},{24,16},{1,9},{9,1},{17,25},{25,17},{2,10},{10... | collective-permute-start | bytes 98312 | tf_op jit(solution)/shard_map/ppermute | solution.py:10
  4.0 59.9 %collective-permute-start.9 = (bf16[128,128]{0,1:T(8,128)(2,1)S(1)}, bf16[128,128]{0,1:T(8,128)(2,1)S(1)}, u32[]{:S(2)}, u32[]{:S(2)}) collective-permute-start(bf16[128,128]{0,1:T(8,128)(2,1)S(1)} %copy.9), channel_id=1, source_target_pairs={{0,4},{1,5},{2,6},{3,7},{4,0},{5,1},{6,2},{7,3},{8,12},{9,13},{10,... | collective-permute-start | bytes 98312 | tf_op jit(solution)/shard_map/ppermute | solution.py:10
  6.6 57.8 %collective-permute-start.5 = (bf16[128,128]{0,1:T(8,128)(2,1)S(1)}, bf16[128,128]{0,1:T(8,128)(2,1)S(1)}, u32[]{:S(2)}, u32[]{:S(2)}) collective-permute-start(bf16[128,128]{0,1:T(8,128)(2,1)S(1)} %copy.9), channel_id=1, source_target_pairs={{0,2},{1,3},{2,0},{3,1},{4,6},{5,7},{6,4},{7,5},{8,10},{9,11},{10,... | collective-permute-start | bytes 98312 | tf_op jit(solution)/shard_map/ppermute | solution.py:10
  9.4 3.6 %collective-permute-start.2 = (bf16[8,128]{1,0:T(8,128)(2,1)S(1)}, bf16[8,128]{1,0:T(8,128)(2,1)S(1)}, u32[]{:S(2)}, u32[]{:S(2)}) collective-permute-start(bf16[8,128]{1,0:T(8,128)(2,1)S(1)} %get-tuple-element.39), channel_id=1, source_target_pairs={{0,1},{1,0},{2,3},{3,2},{4,5},{5,4},{6,7},{7,6},{8,9},{9,8},{10,11... | collective-permute-start | bytes 6152 | tf_op jit(solution)/shard_map/ppermute | solution.py:10
  13.0 3.6 %collective-permute-start.3 = (bf16[8,128]{1,0:T(8,128)(2,1)S(1)}, bf16[8,128]{1,0:T(8,128)(2,1)S(1)}, u32[]{:S(2)}, u32[]{:S(2)}) collective-permute-start(bf16[8,128]{1,0:T(8,128)(2,1)S(1)} %get-tuple-element.23), channel_id=1, source_target_pairs={{0,1},{1,0},{2,3},{3,2},{4,5},{5,4},{6,7},{7,6},{8,9},{9,8},{10,11... | collective-permute-start | bytes 6152 | tf_op jit(solution)/shard_map/ppermute | solution.py:10
  16.6 3.6 %collective-permute-start.6 = (bf16[16,128]{1,0:T(8,128)(2,1)S(1)}, bf16[16,128]{1,0:T(8,128)(2,1)S(1)}, u32[]{:S(2)}, u32[]{:S(2)}) collective-permute-start(bf16[16,128]{1,0:T(8,128)(2,1)S(1)} %pad_maximum_fusion.4), channel_id=1, source_target_pairs={{0,2},{1,3},{2,0},{3,1},{4,6},{5,7},{6,4},{7,5},{8,10},{9,11},{10,... | collective-permute-start | bytes 12296 | tf_op jit(solution)/shard_map/ppermute | solution.py:10
  20.2 3.6 %collective-permute-start.7 = (bf16[16,128]{1,0:T(8,128)(2,1)S(1)}, bf16[16,128]{1,0:T(8,128)(2,1)S(1)}, u32[]{:S(2)}, u32[]{:S(2)}) collective-permute-start(bf16[16,128]{1,0:T(8,128)(2,1)S(1)} %pad_maximum_fusion.5), channel_id=1, source_target_pairs={{0,2},{1,3},{2,0},{3,1},{4,6},{5,7},{6,4},{7,5},{8,10},{9,11},{10,... | collective-permute-start | bytes 12296 | tf_op jit(solution)/shard_map/ppermute | solution.py:10
  23.8 4.5 %collective-permute-start.10 = (bf16[32,128]{1,0:T(8,128)(2,1)S(1)}, bf16[32,128]{1,0:T(8,128)(2,1)S(1)}, u32[]{:S(2)}, u32[]{:S(2)}) collective-permute-start(bf16[32,128]{1,0:T(8,128)(2,1)S(1)} %pad_maximum_fusion.2), channel_id=1, source_target_pairs={{0,4},{1,5},{2,6},{3,7},{4,0},{5,1},{6,2},{7,3},{8,12},{9,13},{10,... | collective-permute-start | bytes 24584 | tf_op jit(solution)/shard_map/ppermute | solution.py:10
  28.3 4.5 %collective-permute-start.11 = (bf16[32,128]{1,0:T(8,128)(2,1)S(1)}, bf16[32,128]{1,0:T(8,128)(2,1)S(1)}, u32[]{:S(2)}, u32[]{:S(2)}) collective-permute-start(bf16[32,128]{1,0:T(8,128)(2,1)S(1)} %pad_maximum_fusion.3), channel_id=1, source_target_pairs={{0,4},{1,5},{2,6},{3,7},{4,0},{5,1},{6,2},{7,3},{8,12},{9,13},{10,... | collective-permute-start | bytes 24584 | tf_op jit(solution)/shard_map/ppermute | solution.py:10
  32.9 1.2 %collective-permute-start.14 = (bf16[64,128]{1,0:T(8,128)(2,1)S(1)}, bf16[64,128]{1,0:T(8,128)(2,1)S(1)}, u32[]{:S(2)}, u32[]{:S(2)}) collective-permute-start(bf16[64,128]{1,0:T(8,128)(2,1)S(1)} %pad_maximum_fusion), channel_id=1, source_target_pairs={{0,8},{8,0},{16,24},{24,16},{1,9},{9,1},{17,25},{25,17},{2,10},{10... | collective-permute-start | bytes 49160 | tf_op jit(solution)/shard_map/ppermute | solution.py:10
  34.1 1.2 %collective-permute-start.15 = (bf16[64,128]{1,0:T(8,128)(2,1)S(1)}, bf16[64,128]{1,0:T(8,128)(2,1)S(1)}, u32[]{:S(2)}, u32[]{:S(2)}) collective-permute-start(bf16[64,128]{1,0:T(8,128)(2,1)S(1)} %pad_maximum_fusion.1), channel_id=1, source_target_pairs={{0,8},{8,0},{16,24},{24,16},{1,9},{9,1},{17,25},{25,17},{2,10},{10... | collective-permute-start | bytes 49160 | tf_op jit(solution)/shard_map/ppermute | solution.py:10
  35.3 1.2 %collective-permute-start.12 = (bf16[128,128]{1,0:T(8,128)(2,1)S(1)}, bf16[128,128]{1,0:T(8,128)(2,1)S(1)}, u32[]{:S(2)}, u32[]{:S(2)}) collective-permute-start(bf16[128,128]{1,0:T(8,128)(2,1)S(1)} %copy-done.2), channel_id=1, source_target_pairs={{0,8},{8,0},{16,24},{24,16},{1,9},{9,1},{17,25},{25,17},{2,10},{10... | collective-permute-start | bytes 98312 | tf_op jit(solution)/shard_map/ppermute | solution.py:10
  36.5 3.9 %collective-permute-start.16 = (bf16[128,128]{1,0:T(8,128)(2,1)S(1)}, bf16[128,128]{1,0:T(8,128)(2,1)S(1)}, u32[]{:S(2)}, u32[]{:S(2)}) collective-permute-start(bf16[128,128]{1,0:T(8,128)(2,1)S(1)} %copy-done.2), channel_id=1, source_target_pairs={{0,16},{8,24},{16,0},{24,8},{1,17},{9,25},{17,1},{25,9},{2,18},{10... | collective-permute-start | bytes 98312 | tf_op jit(solution)/shard_map/ppermute | solution.py:10
  40.4 3.9 %collective-permute-start = (bf16[128,128]{1,0:T(8,128)(2,1)S(1)}, bf16[128,128]{1,0:T(8,128)(2,1)S(1)}, u32[]{:S(2)}, u32[]{:S(2)}) collective-permute-start(bf16[128,128]{1,0:T(8,128)(2,1)S(1)} %copy-done.2), channel_id=1, source_target_pairs={{0,1},{1,0},{2,3},{3,2},{4,5},{5,4},{6,7},{7,6},{8,9},{9,8},{10,11... | collective-permute-start | bytes 98312 | tf_op jit(solution)/shard_map/ppermute | solution.py:10
  44.3 3.9 %collective-permute-start.4 = (bf16[128,128]{1,0:T(8,128)(2,1)S(1)}, bf16[128,128]{1,0:T(8,128)(2,1)S(1)}, u32[]{:S(2)}, u32[]{:S(2)}) collective-permute-start(bf16[128,128]{1,0:T(8,128)(2,1)S(1)} %copy-done.2), channel_id=1, source_target_pairs={{0,2},{1,3},{2,0},{3,1},{4,6},{5,7},{6,4},{7,5},{8,10},{9,11},{10,... | collective-permute-start | bytes 98312 | tf_op jit(solution)/shard_map/ppermute | solution.py:10
  48.2 5.1 %collective-permute-start.8 = (bf16[128,128]{1,0:T(8,128)(2,1)S(1)}, bf16[128,128]{1,0:T(8,128)(2,1)S(1)}, u32[]{:S(2)}, u32[]{:S(2)}) collective-permute-start(bf16[128,128]{1,0:T(8,128)(2,1)S(1)} %copy-done.2), channel_id=1, source_target_pairs={{0,4},{1,5},{2,6},{3,7},{4,0},{5,1},{6,2},{7,3},{8,12},{9,13},{10,... | collective-permute-start | bytes 98312 | tf_op jit(solution)/shard_map/ppermute | solution.py:10
  53.3 3.9 %collective-permute-start.18 = (bf16[128,128]{1,0:T(8,128)(2,1)S(1)}, bf16[128,128]{1,0:T(8,128)(2,1)S(1)}, u32[]{:S(2)}, u32[]{:S(2)}) collective-permute-start(bf16[128,128]{1,0:T(8,128)(2,1)S(1)} %constant_dynamic-update-slice_fusion), channel_id=1, source_target_pairs={{0,16},{8,24},{16,0},{24,8},{1,17},{9,25},{17,1},{25,9},{2,18},{10... | collective-permute-start | bytes 98312 | tf_op jit(solution)/shard_map/ppermute | solution.py:10
  57.2 3.9 %collective-permute-start.19 = (bf16[128,128]{1,0:T(8,128)(2,1)S(1)}, bf16[128,128]{1,0:T(8,128)(2,1)S(1)}, u32[]{:S(2)}, u32[]{:S(2)}) collective-permute-start(bf16[128,128]{1,0:T(8,128)(2,1)S(1)} %constant_dynamic-update-slice_fusion.5), channel_id=1, source_target_pairs={{0,16},{8,24},{16,0},{24,8},{1,17},{9,25},{17,1},{25,9},{2,18},{10... | collective-permute-start | bytes 98312 | tf_op jit(solution)/shard_map/ppermute | solution.py:10
  61.1 3.9 %collective-permute-start.1 = (bf16[128,128]{0,1:T(8,128)(2,1)S(1)}, bf16[128,128]{0,1:T(8,128)(2,1)S(1)}, u32[]{:S(2)}, u32[]{:S(2)}) collective-permute-start(bf16[128,128]{0,1:T(8,128)(2,1)S(1)} %copy.9), channel_id=1, source_target_pairs={{0,1},{1,0},{2,3},{3,2},{4,5},{5,4},{6,7},{7,6},{8,9},{9,8},{10,11... | collective-permute-start | bytes 98312 | tf_op jit(solution)/shard_map/ppermute | solution.py:10
where the time goes:
time: 66.3 us; the launch traced here: 66.2 us
  waiting for transfers between devices  39.8 us (60%)
  starting transfers between devices  17.6 us (27%)
  matrix products  4.87 us (7%)
  local copies, waits for them, and re-layouts  2.91 us (4%)
  other arithmetic  0.69 us (1%)
    ppermute x20, waiting for transfers between devices, from_partner(): return lax.ppermute(value, axis, pairs)  39.8 us
    ppermute x20, starting transfers between devices, from_partner(): return lax.ppermute(value, axis, pairs)  17.6 us
    dot_general x12, matrix products, attend(): jnp.einsum('hqk,kd->qhd', weights.astype(jnp.bfloat16), value_slice, pref...  2.64 us
    dot_general x12, matrix products, attend(): jnp.einsum('qhd,kd->hqk', grouped, key_slice, preferred_element_type=jnp....  2.23 us
  transfers between devices with their start and end apart: 20, of which 16 were waited for; matrix products, arithmetic and copies ran while one was open for 10% of the time, Pallas kernels for 0%

commit v1 on v0

v1 whole, which is shorter than its diff:
```python
import functools
import math

import jax
import jax.numpy as jnp
from jax import lax
from jax.experimental import pallas as pl
from jax.experimental.pallas import tpu as pltpu
from jax.sharding import PartitionSpec as P

MESH = pl.DeviceIdType.MESH
GROUP_ROWS = 512


def dot(a, b, dims):
    return lax.dot_general(a, b, (dims, ((), ())), preferred_element_type=jnp.float32)


def attend(state, stacked, keys, values, factor):
    scores = dot(keys, stacked, ((1,), (1,)))
    fresh = jnp.max(scores, axis=0, keepdims=True)
    if state is not None:
        running, denominator, numerator = state
        fresh = jnp.maximum(running, fresh)
    weights = jnp.exp2((scores - fresh) * factor)
    total = jnp.sum(weights, axis=0, keepdims=True)
    update = dot(values, weights.astype(jnp.bfloat16), ((0,), (0,)))
    if state is not None:
        fade = jnp.exp2((running - fresh) * factor)
        total = denominator * fade + total
        update = numerator * fade + update
    return fresh, total, update


def flipped(index, bit):
    mask = 2**bit
    return index + mask - 2 * mask * lax.rem(lax.div(index, mask), 2)


def kernel(
    n_hi, n_lo, q_hbm, k_hbm, v_hbm, pos_hbm, out_ref,
    q, k, v, pos, slabs, k_in, v_in,
    local_sem, lo_send, lo_recv, hi_send, hi_recv, block_send, block_recv,
):
    hi, lo = lax.axis_index("hi"), lax.axis_index("lo")
    barrier = pltpu.get_barrier_semaphore()
    hi_peer = [lax.rem(hi + d, n_hi) for d in range(n_hi)]
    lo_peer = [lax.rem(lo + d, n_lo) for d in range(n_lo)]
    for d in range(1, n_lo):
        pl.semaphore_signal(barrier, inc=1, device_id={"lo": lo_peer[d]}, device_id_type=MESH)
    for d in range(1, n_hi):
        pl.semaphore_signal(barrier, inc=1, device_id={"hi": hi_peer[d]}, device_id_type=MESH)

    fetches = [
        pltpu.make_async_copy(source, target, local_sem.at[i])
        for i, (source, target) in enumerate(
            [(pos_hbm, pos), (k_hbm, k), (v_hbm, v), (q_hbm, q)]
        )
    ]
    for fetch in fetches:
        fetch.start()
    for fetch in fetches:
        fetch.wait()

    block_rows, width = k.shape
    heads = q.shape[1] // width
    glob = pos.shape[1]
    factor = width**-0.5 * math.log2(math.e)

    row = lax.broadcasted_iota(jnp.int32, (2 * glob, block_rows), 0)
    column = lax.broadcasted_iota(jnp.int32, (2 * glob, block_rows), 1)
    wanted = jnp.zeros_like(row)
    for i in range(glob):
        wanted = jnp.where(lax.rem(row, glob) == i, pos[0, i], wanted)
    one_hot = jnp.where(column == wanted, 1.0, 0.0).astype(jnp.bfloat16)
    picked_k = dot(one_hot, k[...], ((1,), (0,)))
    picked_v = dot(one_hot, v[...], ((1,), (0,)))
    top = lax.broadcasted_iota(jnp.int32, picked_k.shape, 0) < glob
    slabs[0, 0] = jnp.where(top, picked_k, picked_v).astype(jnp.bfloat16)

    stacked = jnp.concatenate([q[:, h * width : (h + 1) * width] for h in range(heads)], axis=0)
    state = attend(None, stacked, k[...], v[...], factor)

    pl.semaphore_wait(barrier, n_lo + n_hi - 2)

    lo_copies = []
    for d in range(1, n_lo):
        copy = pltpu.make_async_remote_copy(
            slabs.at[0, 0], slabs.at[0, d], lo_send.at[d], lo_recv.at[d],
            device_id={"lo": lo_peer[d]}, device_id_type=MESH,
        )
        copy.start()
        lo_copies.append(copy)

    def forward(d):
        for e in range(1, n_hi):
            pltpu.make_async_remote_copy(
                slabs.at[0, d], slabs.at[e, d], hi_send.at[e], hi_recv.at[e],
                device_id={"hi": hi_peer[e]}, device_id_type=MESH,
            ).start()

    forward(0)
    lo_bits, hi_bits = n_lo.bit_length() - 1, n_hi.bit_length() - 1
    partners = [("lo", b) for b in reversed(range(lo_bits))] + [("hi", b) for b in reversed(range(hi_bits))]
    blocks = []
    for j, (axis, bit) in enumerate(partners):
        target = {axis: flipped(lo if axis == "lo" else hi, bit)}
        for i, (source, place) in enumerate([(k, k_in), (v, v_in)]):
            copy = pltpu.make_async_remote_copy(
                source, place.at[j], block_send.at[i, j], block_recv.at[i, j],
                device_id=target, device_id_type=MESH,
            )
            copy.start()
            blocks.append(copy)

    for d in range(1, n_lo):
        lo_copies[d - 1].wait_recv()
        forward(d)

    near = len(partners) - 1
    for copy in blocks[2:]:
        copy.wait_recv()
    state = attend(
        state, stacked,
        k_in[1:].reshape(near * block_rows, width),
        v_in[1:].reshape(near * block_rows, width), factor,
    )

    for copy in blocks[:2]:
        copy.wait_recv()
    group = max(1, GROUP_ROWS // (n_lo * glob))
    for begin in range(0, n_hi, group):
        end = min(begin + group, n_hi)
        for e in range(max(begin, 1), end):
            pltpu.make_async_copy(slabs.at[e], slabs.at[e], hi_recv.at[e]).wait()
        mixed = slabs[begin:end].astype(jnp.float32)
        rows = (end - begin) * n_lo * glob
        keys = mixed[:, :, :glob].reshape(rows, width).astype(jnp.bfloat16)
        values = mixed[:, :, glob:].reshape(rows, width).astype(jnp.bfloat16)
        if begin == 0:
            keys = jnp.concatenate([k_in[0], keys], axis=0)
            values = jnp.concatenate([v_in[0], values], axis=0)
        state = attend(state, stacked, keys, values, factor)

    _, denominator, numerator = state
    result = numerator * (1.0 / denominator)
    for h in range(heads):
        part = result[:, h * block_rows : (h + 1) * block_rows]
        out_ref[:, h * width : (h + 1) * width] = jnp.transpose(part).astype(out_ref.dtype)

    for copy in lo_copies + blocks:
        copy.wait_send()
    for e in range(1, n_hi):
        pltpu.make_async_copy(slabs.at[e], slabs.at[e], hi_send.at[e]).wait()


def local(n_hi, n_lo, queries, key_rows, value_rows, global_positions):
    partners = (n_lo.bit_length() - 1) + (n_hi.bit_length() - 1)
    glob = global_positions.shape[1]
    width = key_rows.shape[1]
    dma = pltpu.SemaphoreType.DMA
    return pl.pallas_call(
        functools.partial(kernel, n_hi, n_lo),
        out_shape=jax.ShapeDtypeStruct(queries.shape, queries.dtype),
        in_specs=[pl.BlockSpec(memory_space=pl.ANY)] * 4,
        out_specs=pl.BlockSpec(memory_space=pltpu.VMEM),
        scratch_shapes=[
            pltpu.VMEM(queries.shape, queries.dtype),
            pltpu.VMEM(key_rows.shape, key_rows.dtype),
            pltpu.VMEM(value_rows.shape, value_rows.dtype),
            pltpu.SMEM(global_positions.shape, global_positions.dtype),
            pltpu.VMEM((n_hi, n_lo, 2 * glob, width), key_rows.dtype),
            pltpu.VMEM((partners,) + key_rows.shape, key_rows.dtype),
            pltpu.VMEM((partners,) + value_rows.shape, value_rows.dtype),
            dma((4,)),
            dma((n_lo,)),
            dma((n_lo,)),
            dma((n_hi,)),
            dma((n_hi,)),
            dma((2, partners)),
            dma((2, partners)),
        ],
        compiler_params=pltpu.CompilerParams(collective_id=0, has_side_effects=True),
    )(queries, key_rows, value_rows, global_positions)


def solution(mesh):
    spec = P(("hi", "lo"), None)
    return jax.shard_map(
        functools.partial(local, mesh.shape["hi"], mesh.shape["lo"]),
        mesh=mesh,
        in_specs=(spec,) * 4,
        out_specs=spec,
        check_vma=False,
    )
```

time: 66.3 us -> 16.1 us (0.24)
  waiting for transfers between devices: 39.8 us -> 0 us
  starting transfers between devices: 17.6 us -> 0 us
  Pallas kernels: 0 us -> 14.4 us
  matrix products: 4.87 us -> 0 us
  local copies, waits for them, and re-layouts: 2.91 us -> 1.57 us
  other arithmetic: 0.69 us -> 0 us
    ppermute x20 -> x0, waiting for transfers between devices: 39.8 us -> none  [from_partner(): return lax.ppermute(value, axis, pairs)]
    ppermute x20 -> x0, starting transfers between devices: 17.6 us -> none  [from_partner(): return lax.ppermute(value, axis, pairs)]
    pallas_call x0 -> x1, Pallas kernels: none -> 14.4 us  [local(): pl.pallas_call(functools.partial(kernel, n_hi, n_lo), out_shape=jax.Shape...]
    dot_general x24 -> x0, matrix products: 4.87 us -> none  [the longest x12 2.64 us: attend(): jnp.einsum('hqk,kd->qhd', weights.astype(jnp.bfloat16), value_slice, pref...]
    gather x2 -> x0, local copies, waits for them, and re-layouts: 1.13 us -> none  [the longest x1 0.57 us: local(): picked_keys = jnp.take(key_rows, global_positions[0], axis=0)]
    convert_element_type x1 -> x0, local copies, waits for them, and re-layouts: 0.77 us -> none  [local(): result.reshape(block_rows, head_count * head_width).astype(jnp.bfloat16)]
    unnamed x15 -> x1, local copies, waits for them, and re-layouts: 0.99 us -> 1.57 us
  transfers between devices with their start and end apart: 20 -> 0, of which waited for: 16 -> 0; matrix products, arithmetic and copies ran while one was open for 10% -> 0% of each run, Pallas kernels for 0% -> 0%
where the time goes in v1:
time: 16.1 us; the launch traced here: 16 us
  Pallas kernels  14.4 us (89%)
  local copies, waits for them, and re-layouts  1.57 us (10%)
    pallas_call x1, Pallas kernels, local(): pl.pallas_call(functools.partial(kernel, n_hi, n_lo), out_shape=jax.Shape...  14.4 us
    unnamed x1, local copies, waits for them, and re-layouts  1.57 us

profile of v1, /device:TPU:0, one launch (start us, length us, event | category | flops | bytes accessed | tf_op | source)
XLA Modules:
  0.0 16.0 jit_solution(17092189781473697039)
XLA Ops:
  0.0 14.4 %shard_map.46 = bf16[128,512]{1,0:T(8,128)(2,1)} custom-call(bf16[128,512]{1,0:T(8,128)(2,1)} %q_hbm.1, bf16[128,128]{1,0:T(8,128)(2,1)} %k_hbm.1, bf16[128,128]{1,0:T(8,128)(2,1)} %v_hbm.1, s32[1,8]{1,0:T(1,128)} %pos_hbm.1), custom_call_target="tpu_custom_call" | custom-call | tf_op jit(solution)/shard_map/pallas_call | solution.py:162
  14.4 1.6 %copy.6 = bf16[128,512]{1,0:T(8,128)(2,1)} copy(bf16[128,512]{1,0:T(8,128)(2,1)} %shard_map.46) | data formatting | bytes 262144

commit v2 on v1

--- a/solution.py
+++ b/solution.py
@@ -32,24 +32,27 @@
     return fresh, total, update
 
 
-def flipped(index, bit):
-    mask = 2**bit
-    return index + mask - 2 * mask * lax.rem(lax.div(index, mask), 2)
+def flipped(index, mask):
+    bit = 1
+    while bit <= mask:
+        if mask & bit:
+            index = index + bit - 2 * bit * lax.rem(lax.div(index, bit), 2)
+        bit *= 2
+    return index
 
 
 def kernel(
     n_hi, n_lo, q_hbm, k_hbm, v_hbm, pos_hbm, out_ref,
     q, k, v, pos, slabs, k_in, v_in,
-    local_sem, lo_send, lo_recv, hi_send, hi_recv, block_send, block_recv,
+    local_sem, far_send, far_recv, near_send, near_recv, block_send, block_recv,
 ):
     hi, lo = lax.axis_index("hi"), lax.axis_index("lo")
     barrier = pltpu.get_barrier_semaphore()
-    hi_peer = [lax.rem(hi + d, n_hi) for d in range(n_hi)]
-    lo_peer = [lax.rem(lo + d, n_lo) for d in range(n_lo)]
-    for d in range(1, n_lo):
-        pl.semaphore_signal(barrier, inc=1, device_id={"lo": lo_peer[d]}, device_id_type=MESH)
-    for d in range(1, n_hi):
-        pl.semaphore_signal(barrier, inc=1, device_id={"hi": hi_peer[d]}, device_id_type=MESH)
+    n_far, n_near = n_lo // 2, n_hi * 2
+    far_peer = [{"lo": flipped(lo, 2 * f)} for f in range(n_far)]
+    near_peer = [{"hi": flipped(hi, e // 2), "lo": flipped(lo, e % 2)} for e in range(n_near)]
+    for peer in far_peer[1:] + near_peer[1:]:
+        pl.semaphore_signal(barrier, inc=1, device_id=peer, device_id_type=MESH)
 
     fetches = [
         pltpu.make_async_copy(source, target, local_sem.at[i])
@@ -81,22 +84,22 @@
     stacked = jnp.concatenate([q[:, h * width : (h + 1) * width] for h in range(heads)], axis=0)
     state = attend(None, stacked, k[...], v[...], factor)
 
-    pl.semaphore_wait(barrier, n_lo + n_hi - 2)
+    pl.semaphore_wait(barrier, n_far + n_near - 2)
 
-    lo_copies = []
-    for d in range(1, n_lo):
+    far_copies = []
+    for f in range(1, n_far):
         copy = pltpu.make_async_remote_copy(
-            slabs.at[0, 0], slabs.at[0, d], lo_send.at[d], lo_recv.at[d],
-            device_id={"lo": lo_peer[d]}, device_id_type=MESH,
+            slabs.at[0, 0], slabs.at[0, f], far_send.at[f], far_recv.at[f],
+            device_id=far_peer[f], device_id_type=MESH,
         )
         copy.start()
-        lo_copies.append(copy)
+        far_copies.append(copy)
 
-    def forward(d):
-        for e in range(1, n_hi):
+    def forward(f):
+        for e in range(1, n_near):
             pltpu.make_async_remote_copy(
-                slabs.at[0, d], slabs.at[e, d], hi_send.at[e], hi_recv.at[e],
-                device_id={"hi": hi_peer[e]}, device_id_type=MESH,
+                slabs.at[0, f], slabs.at[e, f], near_send.at[e], near_recv.at[e],
+                device_id=near_peer[e], device_id_type=MESH,
             ).start()
 
     forward(0)
@@ -104,7 +107,7 @@
     partners = [("lo", b) for b in reversed(range(lo_bits))] + [("hi", b) for b in reversed(range(hi_bits))]
     blocks = []
     for j, (axis, bit) in enumerate(partners):
-        target = {axis: flipped(lo if axis == "lo" else hi, bit)}
+        target = {axis: flipped(lo if axis == "lo" else hi, 2**bit)}
         for i, (source, place) in enumerate([(k, k_in), (v, v_in)]):
             copy = pltpu.make_async_remote_copy(
                 source, place.at[j], block_send.at[i, j], block_recv.at[i, j],
@@ -113,9 +116,9 @@
             copy.start()
             blocks.append(copy)
 
-    for d in range(1, n_lo):
-        lo_copies[d - 1].wait_recv()
-        forward(d)
+    for f in range(1, n_far):
+        far_copies[f - 1].wait_recv()
+        forward(f)
 
     near = len(partners) - 1
     for copy in blocks[2:]:
@@ -128,13 +131,13 @@
 
     for copy in blocks[:2]:
         copy.wait_recv()
-    group = max(1, GROUP_ROWS // (n_lo * glob))
-    for begin in range(0, n_hi, group):
-        end = min(begin + group, n_hi)
+    group = max(1, GROUP_ROWS // (n_far * glob))
+    for begin in range(0, n_near, group):
+        end = min(begin + group, n_near)
         for e in range(max(begin, 1), end):
-            pltpu.make_async_copy(slabs.at[e], slabs.at[e], hi_recv.at[e]).wait()
+            pltpu.make_async_copy(slabs.at[e], slabs.at[e], near_recv.at[e]).wait()
         mixed = slabs[begin:end].astype(jnp.float32)
-        rows = (end - begin) * n_lo * glob
+        rows = (end - begin) * n_far * glob
         keys = mixed[:, :, :glob].reshape(rows, width).astype(jnp.bfloat16)
         values = mixed[:, :, glob:].reshape(rows, width).astype(jnp.bfloat16)
         if begin == 0:
@@ -148,10 +151,10 @@
         part = result[:, h * block_rows : (h + 1) * block_rows]
         out_ref[:, h * width : (h + 1) * width] = jnp.transpose(part).astype(out_ref.dtype)
 
-    for copy in lo_copies + blocks:
+    for copy in far_copies + blocks:
         copy.wait_send()
-    for e in range(1, n_hi):
-        pltpu.make_async_copy(slabs.at[e], slabs.at[e], hi_send.at[e]).wait()
+    for e in range(1, n_near):
+        pltpu.make_async_copy(slabs.at[e], slabs.at[e], near_send.at[e]).wait()
 
 
 def local(n_hi, n_lo, queries, key_rows, value_rows, global_positions):
@@ -162,26 +165,26 @@
     return pl.pallas_call(
         functools.partial(kernel, n_hi, n_lo),
         out_shape=jax.ShapeDtypeStruct(queries.shape, queries.dtype),
-        in_specs=[pl.BlockSpec(memory_space=pl.ANY)] * 4,
+        in_specs=[pl.BlockSpec(memory_space=pltpu.HBM)] * 4,
         out_specs=pl.BlockSpec(memory_space=pltpu.VMEM),
         scratch_shapes=[
             pltpu.VMEM(queries.shape, queries.dtype),
             pltpu.VMEM(key_rows.shape, key_rows.dtype),
             pltpu.VMEM(value_rows.shape, value_rows.dtype),
             pltpu.SMEM(global_positions.shape, global_positions.dtype),
-            pltpu.VMEM((n_hi, n_lo, 2 * glob, width), key_rows.dtype),
+            pltpu.VMEM((2 * n_hi, n_lo // 2, 2 * glob, width), key_rows.dtype),
             pltpu.VMEM((partners,) + key_rows.shape, key_rows.dtype),
             pltpu.VMEM((partners,) + value_rows.shape, value_rows.dtype),
             dma((4,)),
-            dma((n_lo,)),
-            dma((n_lo,)),
-            dma((n_hi,)),
-            dma((n_hi,)),
+            dma((n_lo // 2,)),
+            dma((n_lo // 2,)),
+            dma((2 * n_hi,)),
+            dma((2 * n_hi,)),
             dma((2, partners)),
             dma((2, partners)),
         ],
-        compiler_params=pltpu.CompilerParams(collective_id=0, has_side_effects=True),
-    )(queries, key_rows, value_rows, global_positions)
+        compiler_params=pltpu.CompilerParams(collective_id=0, has_side_effects=True, vmem_limit_bytes=12 * 2**20),
+    )(*(pltpu.with_memory_space_constraint(x, pltpu.HBM) for x in (queries, key_rows, value_rows, global_positions)))
 
 
 def solution(mesh):

time: 16.1 us -> 14.3 us (0.89)
  local copies, waits for them, and re-layouts: 1.57 us -> 0.66 us
  Pallas kernels: 14.4 us -> 13.5 us
    pallas_call x1, Pallas kernels: 14.4 us -> 13.5 us  [local(): pl.pallas_call(functools.partial(kernel, n_hi, n_lo), out_shape=jax.Shape...]
    unnamed x1, local copies, waits for them, and re-layouts: 1.57 us -> 0.66 us
where the time goes in v2:
time: 14.3 us; the launch traced here: 14.1 us
  Pallas kernels  13.5 us (94%)
  local copies, waits for them, and re-layouts  0.66 us (5%)
    pallas_call x1, Pallas kernels, local(): pl.pallas_call(functools.partial(kernel, n_hi, n_lo), out_shape=jax.Shape...  13.5 us
    unnamed x1, local copies, waits for them, and re-layouts  0.66 us

profile of v2, /device:TPU:0, one launch (start us, length us, event | category | flops | bytes accessed | tf_op | source)
XLA Modules:
  0.0 14.1 jit_solution(15622217689187961093)
XLA Ops:
  0.0 13.5 %shard_map.46 = bf16[128,512]{1,0:T(8,128)(2,1)S(1)} custom-call(bf16[128,512]{1,0:T(8,128)(2,1)} %q_hbm.1, bf16[128,128]{1,0:T(8,128)(2,1)} %k_hbm.1, bf16[128,128]{1,0:T(8,128)(2,1)} %v_hbm.1, s32[1,8]{1,0:T(1,128)} %pos_hbm.1), custom_call_target="tpu_custom_call" | custom-call | tf_op jit(solution)/shard_map/pallas_call | solution.py:165
  13.5 0.7 %copy.6 = bf16[128,512]{1,0:T(8,128)(2,1)} copy(bf16[128,512]{1,0:T(8,128)(2,1)S(1)} %shard_map.46) | data formatting | bytes 262144

commit v3 on v2

--- a/solution.py
+++ b/solution.py
@@ -87,18 +87,18 @@
     pl.semaphore_wait(barrier, n_far + n_near - 2)
 
     far_copies = []
-    for f in range(1, n_far):
+    for f in reversed(range(1, n_far)):
         copy = pltpu.make_async_remote_copy(
             slabs.at[0, 0], slabs.at[0, f], far_send.at[f], far_recv.at[f],
             device_id=far_peer[f], device_id_type=MESH,
         )
         copy.start()
-        far_copies.append(copy)
+        far_copies.insert(0, copy)
 
     def forward(f):
-        for e in range(1, n_near):
+        for e in reversed(range(1, n_near)):
             pltpu.make_async_remote_copy(
-                slabs.at[0, f], slabs.at[e, f], near_send.at[e], near_recv.at[e],
+                slabs.at[0, f], slabs.at[e, f], near_send.at[f], near_recv.at[f],
                 device_id=near_peer[e], device_id_type=MESH,
             ).start()
 
@@ -120,29 +120,22 @@
         far_copies[f - 1].wait_recv()
         forward(f)
 
-    near = len(partners) - 1
-    for copy in blocks[2:]:
+    for copy in blocks:
         copy.wait_recv()
+    rows = len(partners) * block_rows
     state = attend(
-        state, stacked,
-        k_in[1:].reshape(near * block_rows, width),
-        v_in[1:].reshape(near * block_rows, width), factor,
+        state, stacked, k_in[...].reshape(rows, width), v_in[...].reshape(rows, width), factor
     )
 
-    for copy in blocks[:2]:
-        copy.wait_recv()
-    group = max(1, GROUP_ROWS // (n_far * glob))
-    for begin in range(0, n_near, group):
-        end = min(begin + group, n_near)
-        for e in range(max(begin, 1), end):
-            pltpu.make_async_copy(slabs.at[e], slabs.at[e], near_recv.at[e]).wait()
-        mixed = slabs[begin:end].astype(jnp.float32)
-        rows = (end - begin) * n_far * glob
+    group = max(1, GROUP_ROWS // (n_near * glob))
+    cuts = list(range(0, n_far - 1, group)) + [n_far - 1, n_far]
+    for begin, end in zip(cuts, cuts[1:]):
+        for f in range(begin, end):
+            pltpu.make_async_copy(slabs.at[1:, f], slabs.at[1:, f], near_recv.at[f]).wait()
+        mixed = slabs[:, begin:end].astype(jnp.float32)
+        rows = (end - begin) * n_near * glob
         keys = mixed[:, :, :glob].reshape(rows, width).astype(jnp.bfloat16)
         values = mixed[:, :, glob:].reshape(rows, width).astype(jnp.bfloat16)
-        if begin == 0:
-            keys = jnp.concatenate([k_in[0], keys], axis=0)
-            values = jnp.concatenate([v_in[0], values], axis=0)
         state = attend(state, stacked, keys, values, factor)
 
     _, denominator, numerator = state
@@ -153,8 +146,8 @@
 
     for copy in far_copies + blocks:
         copy.wait_send()
-    for e in range(1, n_near):
-        pltpu.make_async_copy(slabs.at[e], slabs.at[e], near_send.at[e]).wait()
+    for f in range(n_far):
+        pltpu.make_async_copy(slabs.at[1:, f], slabs.at[1:, f], near_send.at[f]).wait()
 
 
 def local(n_hi, n_lo, queries, key_rows, value_rows, global_positions):
@@ -178,8 +171,8 @@
             dma((4,)),
             dma((n_lo // 2,)),
             dma((n_lo // 2,)),
-            dma((2 * n_hi,)),
-            dma((2 * n_hi,)),
+            dma((n_lo // 2,)),
+            dma((n_lo // 2,)),
             dma((2, partners)),
             dma((2, partners)),
         ],

time: 14.3 us -> 13.9 us (0.972)
  Pallas kernels: 13.5 us -> 13.1 us
    pallas_call x1, Pallas kernels: 13.5 us -> 13.1 us  [local(): pl.pallas_call(functools.partial(kernel, n_hi, n_lo), out_shape=jax.Shape...]
where the time goes in v3:
time: 13.9 us; the launch traced here: 13.8 us
  Pallas kernels  13.1 us (94%)
  local copies, waits for them, and re-layouts  0.66 us (5%)
    pallas_call x1, Pallas kernels, local(): pl.pallas_call(functools.partial(kernel, n_hi, n_lo), out_shape=jax.Shape...  13.1 us
    unnamed x1, local copies, waits for them, and re-layouts  0.66 us

profile of v3, /device:TPU:0, one launch (start us, length us, event | category | flops | bytes accessed | tf_op | source)
XLA Modules:
  0.0 13.8 jit_solution(3863261956385018007)
XLA Ops:
  0.0 13.1 %shard_map.46 = bf16[128,512]{1,0:T(8,128)(2,1)S(1)} custom-call(bf16[128,512]{1,0:T(8,128)(2,1)} %q_hbm.1, bf16[128,128]{1,0:T(8,128)(2,1)} %k_hbm.1, bf16[128,128]{1,0:T(8,128)(2,1)} %v_hbm.1, s32[1,8]{1,0:T(1,128)} %pos_hbm.1), custom_call_target="tpu_custom_call" | custom-call | tf_op jit(solution)/shard_map/pallas_call | solution.py:158
  13.1 0.7 %copy.6 = bf16[128,512]{1,0:T(8,128)(2,1)} copy(bf16[128,512]{1,0:T(8,128)(2,1)S(1)} %shard_map.46) | data formatting | bytes 262144

commit v4 on v3

--- a/solution.py
+++ b/solution.py
@@ -102,7 +102,6 @@
                 device_id=near_peer[e], device_id_type=MESH,
             ).start()
 
-    forward(0)
     lo_bits, hi_bits = n_lo.bit_length() - 1, n_hi.bit_length() - 1
     partners = [("lo", b) for b in reversed(range(lo_bits))] + [("hi", b) for b in reversed(range(hi_bits))]
     blocks = []
@@ -116,8 +115,9 @@
             copy.start()
             blocks.append(copy)
 
-    for f in range(1, n_far):
-        far_copies[f - 1].wait_recv()
+    for f in range(n_far):
+        if f:
+            far_copies[f - 1].wait_recv()
         forward(f)
 
     for copy in blocks:

time: 13.9 us -> 13.9 us (level)
  no operation moved by 1% of the time
where the time goes in v4:
time: 13.9 us; the launch traced here: 13.8 us
  Pallas kernels  13.1 us (94%)
  local copies, waits for them, and re-layouts  0.66 us (5%)
    pallas_call x1, Pallas kernels, local(): pl.pallas_call(functools.partial(kernel, n_hi, n_lo), out_shape=jax.Shape...  13.1 us
    unnamed x1, local copies, waits for them, and re-layouts  0.66 us

profile of v4, /device:TPU:0, one launch (start us, length us, event | category | flops | bytes accessed | tf_op | source)
XLA Modules:
  0.0 13.8 jit_solution(4506427224456767418)
XLA Ops:
  0.0 13.1 %shard_map.46 = bf16[128,512]{1,0:T(8,128)(2,1)S(1)} custom-call(bf16[128,512]{1,0:T(8,128)(2,1)} %q_hbm.1, bf16[128,128]{1,0:T(8,128)(2,1)} %k_hbm.1, bf16[128,128]{1,0:T(8,128)(2,1)} %v_hbm.1, s32[1,8]{1,0:T(1,128)} %pos_hbm.1), custom_call_target="tpu_custom_call" | custom-call | tf_op jit(solution)/shard_map/pallas_call | solution.py:158
  13.1 0.7 %copy.6 = bf16[128,512]{1,0:T(8,128)(2,1)} copy(bf16[128,512]{1,0:T(8,128)(2,1)S(1)} %shard_map.46) | data formatting | bytes 262144
